TPU v7x, 256 devices: a whole 4x4x8 slice. The times are simulated.
256 devices in a mesh: wide: 64 (over z, x, core), narrow: 4 (over y).
Axes of the slice: x: 4, y: 4, z: 8, core: 2. Of those that a mesh axis runs over, the one named last changes fastest.
Arguments:
- snapshot: float32 [512, 16, 512, 128], P('wide', 'narrow'), may hold values from -81 to 81
Outputs:
- core: float32 [256, 16, 512, 128], P(None, 'narrow', 'wide')
- factor: float32 [512, 256], replicated
All inputs are finite; a program needn't handle non-finite values.
Results may differ from a plain program's by a relative error of at most 0.000071.
Values sent between devices are 32-bit elements; how exact they have to be, the bound alone decides.
A program may use at most 320 MiB of HBM per device.

v0:
```python
import jax
import jax.numpy as jnp
from jax import lax
from jax.sharding import PartitionSpec as P

RANK = 256


def on_device(snapshot):
    regrouped = lax.all_to_all(snapshot, "wide", split_axis=2, concat_axis=0, tiled=True)
    rows_all = regrouped.shape[0]
    unfold = regrouped.reshape(rows_all, -1)
    gram = jnp.dot(
        unfold, unfold.T, precision=lax.Precision.HIGHEST, preferred_element_type=jnp.float32
    )
    gram = lax.psum(gram, "narrow")
    gram = lax.psum(gram, "wide")
    upper = jnp.linalg.cholesky(gram).T
    rows_kept = upper[:RANK, :]
    lengths = jnp.sqrt(jnp.sum(rows_kept * rows_kept, axis=1))
    factor = (rows_kept / lengths[:, None]).T
    core = jnp.dot(
        factor.T, unfold, precision=lax.Precision.HIGHEST, preferred_element_type=jnp.float32
    )
    core = core.reshape(RANK, regrouped.shape[1], regrouped.shape[2], regrouped.shape[3])
    return (core, factor)


def solution(mesh):
    in_specs = (P("wide", "narrow", None, None),)
    out_specs = (P(None, "narrow", "wide", None), P())
    return jax.shard_map(
        on_device, mesh=mesh, in_specs=in_specs, out_specs=out_specs, check_vma=False
    )
```

profile of v0, /device:TPU:2, one launch (start us, length us, event | category | flops | bytes accessed | tf_op | source)
XLA Modules:
  0.0 603.6 jit_solution(17001077467662318990)
XLA Ops:
  7.2 8.2 %copy.21 = f32[8,4,512,128]{3,0,1,2:T(8,128)S(1)} copy(f32[8,4,512,128]{3,2,1,0:T(8,128)} %param.1) | data formatting | bytes 16777216 | tf_op args[0]
  15.4 198.1 %all_to_all.15 = f32[8,4,512,128]{3,0,1,2:T(8,128)S(1)} all-to-all(f32[8,4,512,128]{3,0,1,2:T(8,128)S(1)} %copy.21), channel_id=1, replica_groups=mesh['wide'=64,'narrow'=4] {'wide'}, dimensions={2} | all-to-all | bytes 16777216 | tf_op jit(solution)/shard_map/all_to_all | solution.py:10
  213.5 11.3 %copy.32 = f32[8,4,64,8,128]{4,3,1,0,2:T(8,128)} copy(f32[8,4,64,8,128]{4,0,1,3,2:T(8,128)S(1)} %bitcast.42) | data formatting | bytes 16777216 | tf_op jit(solution)/shard_map/all_to_all | solution.py:10
  224.8 9.4 %reshape.40 = f32[512,4096]{1,0:T(8,128)} reshape(f32[64,8,4,8,128]{4,3,2,1,0:T(8,128)} %bitcast.43) | data formatting | bytes 16777216 | tf_op jit(solution)/shard_map/reshape | solution.py:12
  234.2 17.2 %fusion.15 = f32[512,512]{0,1:T(8,128)} fusion(f32[512,4096]{1,0:T(8,128)} %reshape.40), kind=kOutput, calls=%fused_computation.43 | convolution fusion | flops 12884901888 | bytes 9437184 | tf_op jit(solution)/shard_map/dot_general | solution.py:13
  251.5 47.4 %all-reduce.4.cloned.1.call-done = f32[512,512]{0,1:T(8,128)} async-done(((f32[512,512]{0,1:T(8,128)}), f32[512,512]{0,1:T(8,128)}) %all-reduce.4.cloned.1.call-update) | async-done | bytes 1048592 | tf_op jit(solution)/shard_map/psum | solution.py:16
  299.0 9.4 %copy.25 = f32[4096,512]{1,0:T(8,128)} copy(f32[4096,512]{0,1:T(8,128)} %bitcast.40) | data formatting | bytes 16777216 | tf_op jit(solution)/shard_map/dot_general | solution.py:22
  308.4 180.5 %all-reduce.6.cloned.1.call-done = f32[512,512]{0,1:T(8,128)} async-done(((f32[512,512]{0,1:T(8,128)}), f32[512,512]{0,1:T(8,128)}) %all-reduce.6.cloned.1.call-update) | async-done | bytes 1048592 | tf_op jit(solution)/shard_map/psum | solution.py:17
  488.9 1.6 copy.24
  490.4 1.4 fusion
  491.9 11.7 %cholesky.104 = f32[128,128]{1,0:T(8,128)S(1)} custom-call(f32[128,128]{1,0:T(8,128)S(1)} %cholesky.266), custom_call_target="Cholesky" | custom-call | tf_op jit(solution)/shard_map/jit(cholesky)/cholesky | solution.py:18
  503.7 0.1 cholesky.224
  503.8 9.8 %custom-call.27 = f32[1,128,128]{1,2,0:T(8,128)S(1)} custom-call(f32[1,128,128]{2,1,0:T(8,128)S(1)} %get-tuple-element.19), custom_call_target="InvertDiagBlocksLowerTriangular" | custom-call | tf_op jit(solution)/shard_map/jit(cholesky)/cholesky | solution.py:18
  513.6 0.3 constant_dynamic-update-slice_fusion.2
  513.9 0.3 convolution_subtract_fusion
  514.3 11.7 %cholesky.217 = f32[128,128]{1,0:T(8,128)S(1)} custom-call(f32[128,128]{1,0:T(8,128)S(1)} %cholesky.270), custom_call_target="Cholesky" | custom-call | tf_op jit(solution)/shard_map/jit(cholesky)/cholesky | solution.py:18
  526.0 10.0 %custom-call.28 = f32[1,128,128]{1,2,0:T(8,128)S(1)} custom-call(f32[1,128,128]{2,1,0:T(8,128)S(1)} %get-tuple-element.16), custom_call_target="InvertDiagBlocksLowerTriangular" | custom-call | tf_op jit(solution)/shard_map/jit(cholesky)/cholesky | solution.py:18
  536.0 0.3 convolution_dynamic-update-slice_fusion
  536.3 0.4 convolution_subtract_fusion.1
  536.7 11.7 %cholesky.238 = f32[128,128]{1,0:T(8,128)S(1)} custom-call(f32[128,128]{1,0:T(8,128)S(1)} %cholesky.275), custom_call_target="Cholesky" | custom-call | tf_op jit(solution)/shard_map/jit(cholesky)/cholesky | solution.py:18
  548.4 9.8 %custom-call.29 = f32[1,128,128]{1,2,0:T(8,128)S(1)} custom-call(f32[1,128,128]{2,1,0:T(8,128)S(1)} %get-tuple-element.13), custom_call_target="InvertDiagBlocksLowerTriangular" | custom-call | tf_op jit(solution)/shard_map/jit(cholesky)/cholesky | solution.py:18
  558.2 0.2 convolution_dynamic-update-slice_fusion.1
  558.4 0.4 convolution_subtract_fusion.2
  558.8 11.7 %cholesky.255 = f32[128,128]{1,0:T(8,128)S(1)} custom-call(f32[128,128]{1,0:T(8,128)S(1)} %convolution_subtract_fusion.2), custom_call_target="Cholesky" | custom-call | tf_op jit(solution)/shard_map/jit(cholesky)/cholesky | solution.py:18
  570.6 0.6 compare_reduce_fusion.1
  571.2 0.6 compare_reduce_fusion
  571.8 0.6 compare_reduce_fusion.2
  575.0 0.1 select_bitcast_fusion
  575.1 0.3 multiply_reduce_fusion
  575.4 0.9 fusion.7
  576.3 15.8 %fusion.1 = f32[256,4,8,128]{3,0,2,1:T(8,128)S(1)} fusion(f32[4,8,128,512]{3,2,1,0:T(8,128)} %bitcast.41, f32[512,512]{0,1:T(8,128)S(1)} %select_bitcast_fusion, f32[256]{0:T(256)S(1)} %sqrt.7), kind=kOutput, calls=%fused_computation.10 | convolution fusion | flops 6442582016 | bytes 13108224 | tf_op jit(solution)/shard_map/dot_general | solution.py:22
  592.1 4.4 copy.27
  (12 shorter events, 0.3 us)
Async XLA Ops:
  7.2 291.8 %all-reduce.4.cloned.1.call-start = ((), (), s32[]{:S(2)}) async-start(), calls=%async_computation.1 | async-start | bytes 2097152 | tf_op jit(solution)/shard_map/psum | solution.py:16
  251.5 237.4 %all-reduce.6.cloned.1.call-start = ((), (), s32[]{:S(2)}) async-start(), calls=%async_computation.2 | async-start | bytes 2097152 | tf_op jit(solution)/shard_map/psum | solution.py:17
Sparse Core Ops, SparseCore 0:
  251.6 47.3 all-reduce.3
  302.8 186.0 all-reduce.5
where the time goes:
time: 609 us; the launch traced here: 604 us
  waiting for transfers between devices  228 us (37%)
  blocking collectives  198 us (33%)
  other arithmetic  81.2 us (13%)
  local copies, waits for them, and re-layouts  44.5 us (7%)
  matrix products  34.9 us (6%)
  between operations  16.9 us (3%)
    all_to_all x1, blocking collectives, on_device(): lax.all_to_all(snapshot, 'wide', split_axis=2, concat_axis=0, tiled=True)  198 us
    psum x1, waiting for transfers between devices, on_device(): gram = lax.psum(gram, 'wide')  180 us
    another operation x14, other arithmetic, on_device(): upper = jnp.linalg.cholesky(gram).T  78.5 us
    psum x1, waiting for transfers between devices, on_device(): gram = lax.psum(gram, 'narrow')  47.4 us
    dot_general x1, matrix products, on_device(): jnp.dot(unfold, unfold.T, precision=lax.Precision.HIGHEST, preferred_elem...  17.2 us
    dot_general x1, matrix products, on_device(): jnp.dot(factor.T, unfold, precision=lax.Precision.HIGHEST, preferred_elem...  15.8 us
    unnamed x2, local copies, waits for them, and re-layouts  12.7 us
  transfers between devices with their start and end apart: 2, of which 2 were waited for; matrix products, arithmetic and copies ran while one was open for 2% of the time, Pallas kernels for 0%

commit v1 on v0

--- a/solution.py
+++ b/solution.py
@@ -14,7 +14,7 @@
         unfold, unfold.T, precision=lax.Precision.HIGHEST, preferred_element_type=jnp.float32
     )
     gram = lax.psum(gram, "narrow")
-    gram = lax.psum(gram, "wide")
+    gram = jnp.sum(lax.all_gather(gram, "wide"), axis=0)
     upper = jnp.linalg.cholesky(gram).T
     rows_kept = upper[:RANK, :]
     lengths = jnp.sqrt(jnp.sum(rows_kept * rows_kept, axis=1))

time: 609 us -> 680 us (1.12)
  waiting for transfers between devices: 228 us -> 277 us
  other arithmetic: 81.2 us -> 101 us
    all_gather x0 -> x1, waiting for transfers between devices: none -> 230 us  [on_device(): gram = jnp.sum(lax.all_gather(gram, 'wide'), axis=0)]
    psum x1 -> x0, waiting for transfers between devices: 180 us -> none  [on_device(): gram = lax.psum(gram, 'wide')]
    reduce_sum x0 -> x1, other arithmetic: none -> 21.2 us  [on_device(): gram = jnp.sum(lax.all_gather(gram, 'wide'), axis=0)]
  transfers between devices with their start and end apart: 2 -> 2, of which waited for: 2 -> 2; matrix products, arithmetic and copies ran while one was open for 2% -> 1% of each run, Pallas kernels for 0% -> 0%
where the time goes in v1:
time: 680 us; the launch traced here: 672 us
  waiting for transfers between devices  277 us (41%)
  blocking collectives  198 us (29%)
  other arithmetic  101 us (15%)
  local copies, waits for them, and re-layouts  42.9 us (6%)
  matrix products  35 us (5%)
  between operations  17 us (2%)
    all_gather x1, waiting for transfers between devices, on_device(): gram = jnp.sum(lax.all_gather(gram, 'wide'), axis=0)  230 us
    all_to_all x1, blocking collectives, on_device(): lax.all_to_all(snapshot, 'wide', split_axis=2, concat_axis=0, tiled=True)  198 us
    another operation x14, other arithmetic, on_device(): upper = jnp.linalg.cholesky(gram).T  78.5 us
    psum x1, waiting for transfers between devices, on_device(): gram = lax.psum(gram, 'narrow')  47.4 us
    reduce_sum x1, other arithmetic, on_device(): gram = jnp.sum(lax.all_gather(gram, 'wide'), axis=0)  21.2 us
    dot_general x1, matrix products, on_device(): jnp.dot(unfold, unfold.T, precision=lax.Precision.HIGHEST, preferred_elem...  17.3 us
    dot_general x1, matrix products, on_device(): jnp.dot(factor.T, unfold, precision=lax.Precision.HIGHEST, preferred_elem...  15.8 us
  transfers between devices with their start and end apart: 2, of which 2 were waited for; matrix products, arithmetic and copies ran while one was open for 1% of the time, Pallas kernels for 0%

profile of v1, /device:TPU:2, one launch (start us, length us, event | category | flops | bytes accessed | tf_op | source)
XLA Modules:
  0.0 671.8 jit_solution(659521183995401789)
XLA Ops:
  7.2 8.2 %copy.18 = f32[8,4,512,128]{3,0,1,2:T(8,128)S(1)} copy(f32[8,4,512,128]{3,2,1,0:T(8,128)} %param.1) | data formatting | bytes 16777216 | tf_op args[0]
  15.4 198.1 %all_to_all.15 = f32[8,4,512,128]{3,0,1,2:T(8,128)S(1)} all-to-all(f32[8,4,512,128]{3,0,1,2:T(8,128)S(1)} %copy.18), channel_id=1, replica_groups=mesh['wide'=64,'narrow'=4] {'wide'}, dimensions={2} | all-to-all | bytes 16777216 | tf_op jit(solution)/shard_map/all_to_all | solution.py:10
  213.5 11.3 %copy.27 = f32[8,4,64,8,128]{4,3,1,0,2:T(8,128)} copy(f32[8,4,64,8,128]{4,0,1,3,2:T(8,128)S(1)} %bitcast.44) | data formatting | bytes 16777216 | tf_op jit(solution)/shard_map/all_to_all | solution.py:10
  224.8 9.4 %reshape.40 = f32[512,4096]{1,0:T(8,128)} reshape(f32[64,8,4,8,128]{4,3,2,1,0:T(8,128)} %bitcast.45) | data formatting | bytes 16777216 | tf_op jit(solution)/shard_map/reshape | solution.py:12
  234.2 17.3 %convolution_bitcast_fusion = f32[1,512,512]{2,1,0:T(8,128)} fusion(f32[512,4096]{1,0:T(8,128)} %reshape.40), kind=kOutput, calls=%fused_computation.1 | convolution fusion | flops 12884901888 | bytes 9437184 | tf_op jit(solution)/shard_map/dot_general | solution.py:13
  251.6 47.4 %all-reduce.3.cloned.1.call-done = f32[1,512,512]{2,1,0:T(8,128)} async-done(((f32[1,512,512]{2,1,0:T(8,128)}), f32[1,512,512]{2,1,0:T(8,128)}) %all-reduce.3.cloned.1.call-update) | async-done | bytes 1048592 | tf_op jit(solution)/shard_map/psum | solution.py:16
  299.1 9.0 %copy.21 = f32[4096,512]{1,0:T(8,128)} copy(f32[4096,512]{0,1:T(8,128)} %bitcast.42) | data formatting | bytes 16777216 | tf_op jit(solution)/shard_map/dot_general | solution.py:22
  308.1 230.0 %all-gather.2.cloned.1.call-done = f32[64,512,512]{2,1,0:T(8,128)} async-done(((f32[1,512,512]{2,1,0:T(8,128)}), f32[64,512,512]{2,1,0:T(8,128)}) %all-gather.2.cloned.1.call-update) | async-done | bytes 67108880 | tf_op jit(solution)/shard_map/all_gather | solution.py:17
  538.2 21.2 %reduce_sum.18 = f32[512,512]{1,0:T(8,128)S(1)} reduce(f32[64,512,512]{2,1,0:T(8,128)} %all-gather.2.cloned.1.call-done, f32[]{:T(128)} %constant.130.clone.1), dimensions={0}, to_apply=%region_1.0 | reduce | flops 16515072 | bytes 68157440 | tf_op jit(solution)/shard_map/reduce_sum | solution.py:17
  559.4 0.3 copy.20
  559.7 0.2 fusion
  560.0 11.7 %cholesky.104 = f32[128,128]{1,0:T(8,128)S(1)} custom-call(f32[128,128]{1,0:T(8,128)S(1)} %cholesky.266), custom_call_target="Cholesky" | custom-call | tf_op jit(solution)/shard_map/jit(cholesky)/cholesky | solution.py:18
  571.9 9.8 %custom-call.27 = f32[1,128,128]{1,2,0:T(8,128)S(1)} custom-call(f32[1,128,128]{2,1,0:T(8,128)S(1)} %get-tuple-element.19), custom_call_target="InvertDiagBlocksLowerTriangular" | custom-call | tf_op jit(solution)/shard_map/jit(cholesky)/cholesky | solution.py:18
  581.7 0.3 constant_dynamic-update-slice_fusion.2
  582.0 0.3 convolution_subtract_fusion
  582.4 11.7 %cholesky.217 = f32[128,128]{1,0:T(8,128)S(1)} custom-call(f32[128,128]{1,0:T(8,128)S(1)} %cholesky.270), custom_call_target="Cholesky" | custom-call | tf_op jit(solution)/shard_map/jit(cholesky)/cholesky | solution.py:18
  594.1 9.9 %custom-call.28 = f32[1,128,128]{1,2,0:T(8,128)S(1)} custom-call(f32[1,128,128]{2,1,0:T(8,128)S(1)} %get-tuple-element.16), custom_call_target="InvertDiagBlocksLowerTriangular" | custom-call | tf_op jit(solution)/shard_map/jit(cholesky)/cholesky | solution.py:18
  604.0 0.3 convolution_dynamic-update-slice_fusion
  604.3 0.4 convolution_subtract_fusion.1
  604.7 11.7 %cholesky.238 = f32[128,128]{1,0:T(8,128)S(1)} custom-call(f32[128,128]{1,0:T(8,128)S(1)} %cholesky.275), custom_call_target="Cholesky" | custom-call | tf_op jit(solution)/shard_map/jit(cholesky)/cholesky | solution.py:18
  616.5 0.7 compare_reduce_fusion.1
  617.2 9.8 %custom-call.29 = f32[1,128,128]{1,2,0:T(8,128)S(1)} custom-call(f32[1,128,128]{2,1,0:T(8,128)S(1)} %get-tuple-element.13), custom_call_target="InvertDiagBlocksLowerTriangular" | custom-call | tf_op jit(solution)/shard_map/jit(cholesky)/cholesky | solution.py:18
  627.0 0.2 convolution_dynamic-update-slice_fusion.1
  627.2 0.4 convolution_subtract_fusion.2
  627.6 11.7 %cholesky.255 = f32[128,128]{1,0:T(8,128)S(1)} custom-call(f32[128,128]{1,0:T(8,128)S(1)} %convolution_subtract_fusion.2), custom_call_target="Cholesky" | custom-call | tf_op jit(solution)/shard_map/jit(cholesky)/cholesky | solution.py:18
  639.3 0.6 compare_reduce_fusion
  640.0 0.6 compare_reduce_fusion.2
  643.2 0.1 select_bitcast_fusion
  643.3 0.3 multiply_reduce_fusion
  643.6 0.9 fusion.7
  644.5 15.8 %fusion.1 = f32[256,4,8,128]{3,0,2,1:T(8,128)S(1)} fusion(f32[4,8,128,512]{3,2,1,0:T(8,128)} %bitcast.43, f32[512,512]{0,1:T(8,128)S(1)} %select_bitcast_fusion, f32[256]{0:T(256)S(1)} %sqrt.7), kind=kOutput, calls=%fused_computation.11 | convolution fusion | flops 6442582016 | bytes 13108224 | tf_op jit(solution)/shard_map/dot_general | solution.py:22
  660.3 4.4 copy.23
  (13 shorter events, 0.4 us)
Async XLA Ops:
  7.2 291.9 %all-reduce.3.cloned.1.call-start = ((), (), s32[]{:S(2)}) async-start(), calls=%async_computation.1 | async-start | bytes 2097152 | tf_op jit(solution)/shard_map/psum | solution.py:16
  251.6 286.6 %all-gather.2.cloned.1.call-start = ((), (), s32[]{:S(2)}) async-start(), calls=%async_computation.2 | async-start | bytes 68157440 | tf_op jit(solution)/shard_map/all_gather | solution.py:17
Sparse Core Ops, SparseCore 0:
  251.7 47.3 all-reduce.2
  302.2 235.8 all-gather.1
